TPU v7x, 128 devices: a whole 4x4x4 slice. The times are simulated.
128 devices in a mesh: req: 32 (over y, z, core), head: 4 (over x).
Axes of the slice: x: 4, y: 4, z: 4, core: 2. Of those that a mesh axis runs over, the one named last changes fastest.
Arguments:
- queries: bfloat16 [64, 512, 4096], P('req', None, 'head'), may hold values from -16 to 16
- new_keys: bfloat16 [64, 512, 1024], P('req', None, 'head'), may hold values from -16 to 16
- incoming_values: bfloat16 [64, 512, 1024], P('req', None, 'head'), may hold values from -6 to 6
- request_cached_keys: bfloat16 [64, 2048, 1024], P('req', None, 'head'), may hold values from -12 to 12
- request_cached_values: bfloat16 [64, 2048, 1024], P('req', None, 'head'), may hold values from -6 to 6
- cache_lengths: int32 [64], P('req'), may hold values from 1 to 2048, 65536 in all
- out_weight: bfloat16 [4096, 4096], P('head'), may hold values from -0.25 to 0.25
- residual: bfloat16 [512, 64, 4096], P(('req', 'head')), may hold values from -3 to 3
- norm_gain: bfloat16 [4096], replicated, may hold values from 0.5 to 1.5
Outputs:
- hidden: bfloat16 [512, 64, 4096], P(('req', 'head'))
- normed: bfloat16 [512, 64, 4096], P(('req', 'head'))
Inputs may be any that keep to these rules, and one draw needn't show every extreme that they name: Request r's cache holds keys in slots 0 to cache_lengths[r] - 1; in every draw the longest request has exactly 2048.
All inputs are finite; a program needn't handle non-finite values. No bound on the sum of `cache_lengths` on one device may be relied on, other than what follows from the above.
Results may differ from a plain program's by a relative error of at most 0.013.
Values may be sent and summed in bfloat16 or wider, within the bound.
A program may use at most 128 MiB of HBM per device.

v0:
```python
import math

import jax
import jax.numpy as jnp
from jax import lax
from jax.experimental import pallas as pl
from jax.experimental.pallas import tpu as pltpu
from jax.sharding import PartitionSpec as P

HEAD_SIZE = 128


NEGATIVE_FILLER = -1e30
Q_TILE = 512
K_BLOCK = 512
LOG2_SCALE = math.log2(math.e) / math.sqrt(HEAD_SIZE)
BF16, F32 = jnp.bfloat16, jnp.float32


def attention_kernel(length_ref, q_ref, new_k_ref, new_v_ref, key_ref, value_ref, out_ref, values):
    length = length_ref[pl.program_id(0)]
    slots, span = key_ref.shape[1], new_k_ref.shape[1]
    values[:slots, :HEAD_SIZE] = value_ref[0]
    values[slots:, :HEAD_SIZE] = new_v_ref[0]
    values[:, HEAD_SIZE:] = jnp.ones((slots + span, HEAD_SIZE), BF16)
    contract_last = (((1,), (1,)), ((), ()))

    def one_head(start, member):
        columns = pl.ds(pl.multiple_of(member * HEAD_SIZE, HEAD_SIZE), HEAD_SIZE)
        query = q_ref[0, pl.ds(start, Q_TILE), columns]
        blocks = [(True, at, K_BLOCK) for at in range(0, slots, K_BLOCK)]
        blocks.append((False, 0, start + Q_TILE))
        running_max = total = None
        for cached, at, count in blocks:
            keys = key_ref[0, at : at + count] if cached else new_k_ref[0, :count]
            scores = lax.dot_general(query, keys, contract_last, preferred_element_type=F32)
            if cached:
                slot = lax.broadcasted_iota(jnp.int32, (1, count), 1) + at
                scores = scores + jnp.where(slot < length, 0.0, NEGATIVE_FILLER)
            else:
                row = lax.broadcasted_iota(jnp.int32, (Q_TILE, count), 0) + start
                column = lax.broadcasted_iota(jnp.int32, (Q_TILE, count), 1)
                scores = jnp.where(column <= row, scores, NEGATIVE_FILLER)
            block_max = jnp.max(scores, axis=1, keepdims=True)
            new_max = block_max if total is None else jnp.maximum(running_max, block_max)
            weights = jnp.exp2((scores - new_max) * LOG2_SCALE).astype(BF16)
            rows = values[at : at + count] if cached else values[slots : slots + count]
            product = jnp.dot(weights, rows, preferred_element_type=F32)
            if total is None:
                total = product
            else:
                total = total * jnp.exp2((running_max - new_max) * LOG2_SCALE) + product
            running_max = new_max
        attended = total[:, :HEAD_SIZE] / total[:, HEAD_SIZE:]
        out_ref[0, pl.ds(start, Q_TILE), columns] = attended.astype(BF16)

    for start in range(0, span, Q_TILE):

        def two_heads(pair, carried):
            one_head(start, 2 * pair)
            one_head(start, 2 * pair + 1)
            return carried

        lax.fori_loop(0, q_ref.shape[2] // HEAD_SIZE // 2, two_heads, 0)


def attend(queries, new_keys, new_values, cached_keys, cached_values, lengths):
    requests, span, width = queries.shape
    slots = cached_keys.shape[1]
    key_heads = new_keys.shape[2] // HEAD_SIZE
    group_width = width // key_heads

    def block(rows, columns):
        return pl.BlockSpec((1, rows, columns), lambda r, g, _: (r, 0, g))

    return pl.pallas_call(
        attention_kernel,
        grid_spec=pltpu.PrefetchScalarGridSpec(
            num_scalar_prefetch=1,
            grid=(requests, key_heads),
            in_specs=[
                block(span, group_width),
                block(span, HEAD_SIZE),
                block(span, HEAD_SIZE),
                block(slots, HEAD_SIZE),
                block(slots, HEAD_SIZE),
            ],
            out_specs=block(span, group_width),
            scratch_shapes=[pltpu.VMEM((slots + span, 2 * HEAD_SIZE), BF16)],
        ),
        out_shape=jax.ShapeDtypeStruct(queries.shape, BF16),
        compiler_params=pltpu.CompilerParams(vmem_limit_bytes=60 << 20),
    )(lengths, queries, new_keys, new_values, cached_keys, cached_values)


def row_product(flat_rows, out_weight):
    return jnp.dot(flat_rows, out_weight, preferred_element_type=jnp.float32)


def body(
    queries,
    new_keys,
    incoming_values,
    request_cached_keys,
    request_cached_values,
    cache_lengths,
    out_weight,
    residual,
    norm_gain,
):
    req_local, span_len, query_width = queries.shape
    attended = attend(
        queries,
        new_keys,
        incoming_values,
        request_cached_keys,
        request_cached_values,
        cache_lengths,
    )
    req_count = lax.axis_size("req")
    head_count = lax.axis_size("head")
    piece_len = span_len // (req_count * head_count)
    share_rows = req_count * piece_len * req_local
    arranged = attended.reshape(req_local, req_count, head_count, piece_len, query_width).transpose(
        2, 1, 3, 0, 4
    )
    flat_rows = arranged.reshape(head_count * share_rows, query_width)
    summed = lax.psum_scatter(
        row_product(flat_rows, out_weight).astype(jnp.bfloat16),
        "head",
        scatter_dimension=0,
        tiled=True,
    )
    exchanged = lax.all_to_all(
        summed.reshape(req_count, piece_len, req_local, -1),
        "req",
        split_axis=0,
        concat_axis=2,
        tiled=True,
    )
    attn_rows = exchanged.reshape(piece_len, req_count * req_local, -1)
    summed_rows = residual.astype(jnp.float32) + lax.optimization_barrier(attn_rows).astype(
        jnp.float32
    )
    hidden = summed_rows.astype(jnp.bfloat16)
    mean_square = jnp.mean(summed_rows * summed_rows, axis=-1, keepdims=True)
    normed = (summed_rows * lax.rsqrt(mean_square + 1e-05) * norm_gain.astype(jnp.float32)).astype(
        jnp.bfloat16
    )
    return (hidden, normed)


def solution(mesh):
    placed = (
        P("req", None, "head"),
        P("req", None, "head"),
        P("req", None, "head"),
        P("req", None, "head"),
        P("req", None, "head"),
        P("req"),
        P("head", None),
        P(("req", "head"), None, None),
        P(),
    )
    return jax.shard_map(
        body,
        mesh=mesh,
        in_specs=placed,
        out_specs=(P(("req", "head"), None, None), P(("req", "head"), None, None)),
        check_vma=False,
    )
```

profile of v0, /device:TPU:1, one launch (start us, length us, event | category | flops | bytes accessed | tf_op | source)
XLA Modules:
  0.0 206.8 jit_solution(8247264119644100506)
XLA Ops:
  7.2 0.0 reduce-scatter.2.cloned.1.call-start
  7.2 31.6 %shard_map.104 = bf16[2,512,1024]{2,1,0:T(8,128)(2,1)} custom-call(s32[2]{0:T(128)} %length_ref.1, bf16[2,512,1024]{2,1,0:T(8,128)(2,1)} %q_ref.1, bf16[2,512,256]{2,1,0:T(8,128)(2,1)} %new_k_ref.1, bf16[2,512,256]{2,1,0:T(8,128)(2,1)} %new_v_ref.1, bf16[2,2048,256]{2,1,0:T(8,128)(2,1)} %key_ref.1, bf16[2,2048,256]{2,1,0:T(8,128)(2,1)} %value_ref.1), custom_call_target="tpu_custom_call" | custom-call | tf_op jit(solution)/shard_map/pallas_call | solution.py:76
  38.8 2.7 %reshape.26 = bf16[2,32,4,4,1024]{4,3,2,1,0:T(4,128)(2,1)S(1)} reshape(bf16[2,512,1024]{2,1,0:T(8,128)(2,1)} %shard_map.104) | data formatting | bytes 4194304 | tf_op jit(solution)/shard_map/reshape | solution.py:124
  41.5 4.6 %copy.15 = bf16[2,32,4,4,1024]{4,0,3,1,2:T(2,128)(2,1)} copy(bf16[2,32,4,4,1024]{4,3,2,1,0:T(4,128)(2,1)S(1)} %reshape.26) | data formatting | bytes 4194304 | tf_op jit(solution)/shard_map/reshape | solution.py:124
  46.1 2.7 %reshape.27 = bf16[1024,1024]{1,0:T(8,128)(2,1)S(1)} reshape(bf16[4,32,4,2,1024]{4,3,2,1,0:T(2,128)(2,1)} %bitcast.9) | data formatting | bytes 4194304 | tf_op jit(solution)/shard_map/reshape | solution.py:127
  48.9 14.2 %convolution_convert_fusion = bf16[1024,4096]{1,0:T(8,128)(2,1)} fusion(bf16[1024,1024]{1,0:T(8,128)(2,1)S(1)} %reshape.27, bf16[1024,4096]{1,0:T(8,128)(2,1)} %param.15), kind=kOutput, calls=%fused_computation | convolution fusion | flops 8594128896 | bytes 18874368 | tf_op jit(solution)/shard_map/dot_general | solution.py:97
  63.1 0.0 reduce-scatter.2.cloned.1.call-update
  63.1 83.9 %reduce-scatter.2.cloned.1.call-done = bf16[256,4096]{1,0:T(8,128)(2,1)} async-done(((bf16[1024,4096]{1,0:T(8,128)(2,1)}), bf16[256,4096]{1,0:T(8,128)(2,1)}) %reduce-scatter.2.cloned.1.call-update) | async-done | bytes 2097168 | tf_op jit(solution)/shard_map/reduce_scatter | solution.py:128
  147.0 4.4 %reshape.28 = bf16[32,4,2,4096]{3,2,1,0:T(2,128)(2,1)} reshape(bf16[256,4096]{1,0:T(8,128)(2,1)} %reduce-scatter.2.cloned.1.call-done) | data formatting | bytes 4194304 | tf_op jit(solution)/shard_map/reshape | solution.py:135
  151.4 0.0 copy-start.1
  151.4 7.8 %all-to-all-start = ((bf16[32,4,2,4096]{3,2,1,0:T(2,128)(2,1)}), bf16[32,4,2,4096]{3,2,1,0:T(2,128)(2,1)S(1)}, u32[]{:S(2)}, u32[]{:S(2)}) async-start(bf16[32,4,2,4096]{3,2,1,0:T(2,128)(2,1)} %reshape.28), calls=%async_computation.1 | async-start | bytes 4194304 | tf_op jit(solution)/shard_map/all_to_all | solution.py:134
  159.2 0.0 copy-done.1
  159.2 28.3 %all-to-all-done = bf16[32,4,2,4096]{3,2,1,0:T(2,128)(2,1)S(1)} async-done(((bf16[32,4,2,4096]{3,2,1,0:T(2,128)(2,1)}), bf16[32,4,2,4096]{3,2,1,0:T(2,128)(2,1)S(1)}, u32[]{:S(2)}, u32[]{:S(2)}) %all-to-all-start) | async-done | bytes 2097184 | tf_op jit(solution)/shard_map/all_to_all | solution.py:134
  187.5 3.9 %copy.13 = bf16[1,4,32,2,4096]{4,3,2,1,0:T(2,128)(2,1)} copy(bf16[1,4,32,2,4096]{4,3,1,2,0:T(2,128)(2,1)S(1)} %bitcast.8) | data formatting | bytes 4194304 | tf_op jit(solution)/shard_map/all_to_all | solution.py:134
  191.4 2.7 %reshape.29 = bf16[4,64,4096]{2,1,0:T(8,128)(2,1)S(1)} reshape(bf16[1,4,32,2,4096]{4,3,2,1,0:T(2,128)(2,1)} %copy.13) | data formatting | bytes 4194304 | tf_op jit(solution)/shard_map/reshape | solution.py:141
  194.1 0.0 copy-start
  194.1 2.5 %multiply_reduce_fusion = f32[4,64]{1,0:T(4,128)S(1)} fusion(bf16[4,64,4096]{2,1,0:T(8,128)(2,1)S(1)} %reshape.29, bf16[4,64,4096]{2,1,0:T(8,128)(2,1)} %param.16), kind=kLoop, calls=%fused_computation.2 | loop fusion | flops 5242624 | bytes 4195328 | tf_op jit(solution)/shard_map/reduce_sum | solution.py:146
  196.6 0.0 copy-done
  196.6 3.3 %multiply_convert_fusion = (bf16[4,64,4096]{2,1,0:T(8,128)(2,1)}, bf16[4,64,4096]{2,1,0:T(8,128)(2,1)}) fusion(bf16[4,64,4096]{2,1,0:T(8,128)(2,1)S(1)} %reshape.29, bf16[4,64,4096]{2,1,0:T(8,128)(2,1)S(1)} %copy-done, f32[4096]{0:T(1024)S(1)} %convert_element_type.22, f32[4,64]{1,0:T(4,128)S(1)} %add_rsqrt_fusion), kind=kLoop, calls=%fused_computation.1 | loop fusion | flops 7340032 | bytes 8406016 | tf_op jit(solution)/shard_map/convert_element_type | solution.py:147
  (2 shorter events, 0.0 us)
Async XLA Ops:
  7.2 139.8 %reduce-scatter.2.cloned.1.call-start = ((), (), s32[]{:S(2)}) async-start(), calls=%async_computation.2 | async-start | bytes 10485760 | tf_op jit(solution)/shard_map/reduce_scatter | solution.py:128
  151.4 7.8 %copy-start.1 = (bf16[4096]{0:T(1024)(128)(2,1)S(1)}, bf16[4096]{0:T(1024)(128)(2,1)}, u32[]{:S(2)}) copy-start(bf16[4096]{0:T(1024)(128)(2,1)} %param.17) | copy-start | bytes 24580
  151.4 36.1 %all-to-all-start = ((bf16[32,4,2,4096]{3,2,1,0:T(2,128)(2,1)}), bf16[32,4,2,4096]{3,2,1,0:T(2,128)(2,1)S(1)}, u32[]{:S(2)}, u32[]{:S(2)}) async-start(bf16[32,4,2,4096]{3,2,1,0:T(2,128)(2,1)} %reshape.28), calls=%async_computation.1 | async-start | bytes 4194304 | tf_op jit(solution)/shard_map/all_to_all | solution.py:134
  194.1 2.5 %copy-start = (bf16[4,64,4096]{2,1,0:T(8,128)(2,1)S(1)}, bf16[4,64,4096]{2,1,0:T(8,128)(2,1)}, u32[]{:S(2)}) copy-start(bf16[4,64,4096]{2,1,0:T(8,128)(2,1)} %param.16) | copy-start | bytes 6291460
Sparse Core Ops, SparseCore 0:
  63.2 83.7 reduce-scatter.1
where the time goes:
time: 207 us
  waiting for transfers between devices  112 us (54%)
  Pallas kernels  31.6 us (15%)
  local copies, waits for them, and re-layouts  21.1 us (10%)
  matrix products  14.2 us (7%)
  between operations  14.1 us (7%)
  starting transfers between devices  7.82 us (4%)
  other arithmetic  5.81 us (3%)
    reduce_scatter x1, waiting for transfers between devices, body(): lax.psum_scatter(row_product(flat_rows, out_weight).astype(jnp.bfloat16),...  83.9 us
    pallas_call x1, Pallas kernels, attend(): pl.pallas_call(attention_kernel, grid_spec=pltpu.PrefetchScalarGridSpec(n...  31.6 us
    all_to_all x1, waiting for transfers between devices, body(): lax.all_to_all(summed.reshape(req_count, piece_len, req_local, -1), 'req'...  28.3 us
    dot_general x1, matrix products, row_product(): return jnp.dot(flat_rows, out_weight, preferred_element_type=jnp.float32)  14.2 us
    all_to_all x1, starting transfers between devices, body(): lax.all_to_all(summed.reshape(req_count, piece_len, req_local, -1), 'req'...  7.79 us
    reshape x2, local copies, waits for them, and re-layouts, body(): attended.reshape(req_local, req_count, head_count, piece_len, query_width)  7.29 us
    reshape x1, local copies, waits for them, and re-layouts, body(): summed.reshape(req_count, piece_len, req_local, -1)  4.38 us
  transfers between devices with their start and end apart: 2, of which 2 were waited for; matrix products, arithmetic and copies ran while one was open for 0% of the time, Pallas kernels for 0%

commit v1 on v0

v1 whole, which is shorter than its diff:
```python
import functools
import math

import jax
import jax.numpy as jnp
from jax import lax
from jax.experimental import pallas as pl
from jax.experimental.pallas import tpu as pltpu
from jax.sharding import PartitionSpec as P

HEAD_SIZE = 128
NEGATIVE_FILLER = -1e30
K_BLOCK = 512
N_TILE = 512
LOG2_SCALE = math.log2(math.e) / math.sqrt(HEAD_SIZE)
BF16, F32 = jnp.bfloat16, jnp.float32
MESH = pl.DeviceIdType.MESH


def spread_kernel(
    sizes,
    length_ref,
    q_hbm,
    new_k_hbm,
    new_v_hbm,
    key_hbm,
    value_hbm,
    weight_hbm,
    gathered,
    query,
    new_keys,
    keys,
    values,
    weight,
    attended,
    rows_of_owner,
    part,
    far_in,
    near_in,
    summed,
    load_sem,
    far_send,
    far_recv,
    near_send,
    near_recv,
    out_send,
    out_recv,
    self_sem,
):
    req_count, head_count, requests, key_heads, members = sizes
    row = lax.axis_index("req")
    me = lax.axis_index("head")
    right = lax.rem(me + 1, head_count)
    left = lax.rem(me + head_count - 1, head_count)
    opposite = lax.rem(me + 2, head_count)
    chunks = part.shape[0]
    slots, span = key_hbm.shape[1], new_k_hbm.shape[1]
    width = weight.shape[1]
    half = width // 2
    lane_groups = [pl.ds(g * HEAD_SIZE, HEAD_SIZE) for g in range(key_heads)]

    barrier = pltpu.get_barrier_semaphore()
    for neighbour in (left, right):
        pl.semaphore_signal(barrier, inc=1, device_id=(row, neighbour), device_id_type=MESH)

    def greet(step, carried):
        peer = lax.rem(row + step, req_count)
        pl.semaphore_signal(barrier, inc=1, device_id=(peer, me), device_id_type=MESH)
        return carried

    lax.fori_loop(1, req_count, greet, 0)

    for r in range(requests):
        for g in range(key_heads):
            values[r, g, :, HEAD_SIZE:] = jnp.ones((slots + span, HEAD_SIZE), BF16)

    loads = []

    def load(source, target):
        copy = pltpu.make_async_copy(source, target, load_sem.at[len(loads)])
        copy.start()
        loads.append(copy)

    for r in range(requests):
        load(q_hbm.at[r], query.at[r])
        load(key_hbm.at[r], keys.at[r])
        load(new_k_hbm.at[r], new_keys.at[r])
        for g, lanes in enumerate(lane_groups):
            load(value_hbm.at[r, :, lanes], values.at[r, g, pl.ds(0, slots), pl.ds(0, HEAD_SIZE)])
            load(new_v_hbm.at[r, :, lanes], values.at[r, g, pl.ds(slots, span), pl.ds(0, HEAD_SIZE)])
    load(weight_hbm, weight)
    per_request = (len(loads) - 1) // requests

    contract_last = (((1,), (1,)), ((), ()))

    def attend(turn, r):
        length = length_ref[r]
        tile = query.shape[1] * 16
        stacked = members * tile
        for g in range(key_heads):
            block = query[r, :, pl.ds(pl.multiple_of(turn * 16, 16), 16), pl.ds(g * members * HEAD_SIZE, members * HEAD_SIZE)]
            block = block.reshape(tile, members * HEAD_SIZE)
            q = jnp.concatenate(
                [block[:, j * HEAD_SIZE : (j + 1) * HEAD_SIZE] for j in range(members)], axis=0
            )
            running_max = total = None
            for at in range(0, slots + span, K_BLOCK):
                cached = at < slots
                if cached:
                    k = keys[r, at : at + K_BLOCK, g * HEAD_SIZE : (g + 1) * HEAD_SIZE]
                else:
                    k = new_keys[r, at - slots : at - slots + K_BLOCK, g * HEAD_SIZE : (g + 1) * HEAD_SIZE]
                scores = lax.dot_general(q, k, contract_last, preferred_element_type=F32)
                if cached:
                    slot = lax.broadcasted_iota(jnp.int32, (1, K_BLOCK), 1) + at
                    scores = scores + jnp.where(slot < length, 0.0, NEGATIVE_FILLER)
                else:
                    line = lax.broadcasted_iota(jnp.int32, (stacked, K_BLOCK), 0)
                    position = ((line >> 4) & 7) * 64 + (line & 15) + turn * 16
                    column = lax.broadcasted_iota(jnp.int32, (stacked, K_BLOCK), 1) + (at - slots)
                    scores = jnp.where(column <= position, scores, NEGATIVE_FILLER)
                block_max = jnp.max(scores, axis=1, keepdims=True)
                new_max = block_max if total is None else jnp.maximum(running_max, block_max)
                weights = jnp.exp2((scores - new_max) * LOG2_SCALE).astype(BF16)
                product = jnp.dot(weights, values[r, g, at : at + K_BLOCK], preferred_element_type=F32)
                if total is None:
                    total = product
                else:
                    total = total * jnp.exp2((running_max - new_max) * LOG2_SCALE) + product
                running_max = new_max
            out = total[:, :HEAD_SIZE] / total[:, HEAD_SIZE:]
            for j in range(members):
                at = (g * members + j) * HEAD_SIZE
                attended[r, :, at : at + HEAD_SIZE] = out[j * tile : (j + 1) * tile]

    def order_rows():
        count = attended.shape[1] // 8
        shape = (count, 8, attended.shape[2])
        first, second = attended[0].reshape(shape), attended[1].reshape(shape)
        upper = lax.broadcasted_iota(jnp.int32, shape, 1) < 4
        even = jnp.where(upper, first, pltpu.roll(second, 4, 1))
        odd = jnp.where(upper, pltpu.roll(first, 4, 1), second)
        for low, rows in enumerate((even, odd)):
            split = rows.reshape(count // 2, 2, 8, shape[2])
            for high in range(2):
                owner = 2 * high + low
                lines = split[:, high].reshape(count * 4, shape[2]).astype(BF16)
                rows_of_owner[owner * count * 4 : (owner + 1) * count * 4] = lines

    def project(c, first):
        def tile(n, carried):
            columns = pl.ds(pl.multiple_of(n * N_TILE, N_TILE), N_TILE)
            product = jnp.dot(rows_of_owner[...], weight[:, columns], preferred_element_type=F32)
            part[c, :, :, columns] = product.astype(BF16).reshape(head_count, -1, N_TILE)
            return carried

        tiles = half // N_TILE
        lax.fori_loop(first * tiles, (first + 1) * tiles, tile, 0)

    def far(c, side):
        return pltpu.make_async_remote_copy(
            src_ref=part.at[c, opposite, :, pl.ds(side * half, half)],
            dst_ref=far_in.at[c, side],
            send_sem=far_send.at[c, side],
            recv_sem=far_recv.at[c, side],
            device_id=(row, (right, left)[side]),
            device_id_type=MESH,
        )

    def near(c, side):
        target = (right, left)[side]
        return pltpu.make_async_remote_copy(
            src_ref=part.at[c, target],
            dst_ref=near_in.at[c, side],
            send_sem=near_send.at[c, side],
            recv_sem=near_recv.at[c, side],
            device_id=(row, target),
            device_id_type=MESH,
        )

    def pass_on(c):
        for side, target in enumerate((right, left)):
            far(c, side).wait_recv()
            columns = pl.ds(side * half, half)
            own = part[c, target, :, columns].astype(F32)
            part[c, target, :, columns] = (own + far_in[c, side].astype(F32)).astype(BF16)
            near(c, side).start()

    group, place = row // chunks, lax.rem(row, chunks)
    groups = req_count // chunks

    def finish(c):
        for side in range(2):
            near(c, side).wait_recv()
        total = part[c, me].astype(F32) + near_in[c, 0].astype(F32) + near_in[c, 1].astype(F32)
        summed[c] = total.reshape(summed.shape[1:]).astype(BF16)

        def send(step, carried):
            outgoing(c, step).start()
            return carried

        if c == 0:
            keep().start()
        lax.fori_loop(1 if c == 0 else 0, groups, send, 0)

    def outgoing(c, step):
        block = lax.rem(group + step, groups)
        target = block * chunks + lax.rem(place + c, chunks)
        return pltpu.make_async_remote_copy(
            src_ref=summed.at[c, block],
            dst_ref=gathered.at[pl.ds(pl.multiple_of(row * 8, 8), 8)],
            send_sem=out_send.at[c, step],
            recv_sem=out_recv.at[row],
            device_id=(target, me),
            device_id_type=MESH,
        )

    def keep():
        lines = gathered.at[pl.ds(pl.multiple_of(row * 8, 8), 8)]
        return pltpu.make_async_copy(summed.at[0, group], lines, self_sem)

    for c in range(chunks):
        turn = lax.rem(place + c, chunks)
        for r in range(requests):
            if c == 0:
                for copy in loads[r * per_request : (r + 1) * per_request]:
                    copy.wait()
            attend(turn, r)
            if c > 0 and r == 0:
                pass_on(c - 1)
        if c > 1:
            finish(c - 2)
        order_rows()
        if c == 0:
            loads[-1].wait()
            pl.semaphore_wait(barrier, 2 + req_count - 1)
        for side in range(2):
            project(c, side)
            far(c, side).start()
    pass_on(chunks - 1)
    for c in range(max(0, chunks - 2), chunks):
        finish(c)

    keep().wait()
    for c in range(chunks):
        for side in range(2):
            far(c, side).wait_send()
            near(c, side).wait_send()

        def sent(step, carried, c=c):
            outgoing(c, step).wait_send()
            return carried

        lax.fori_loop(1 if c == 0 else 0, groups, sent, 0)

    def arrived(step, carried):
        source = lax.rem(row + step, req_count)
        lines = gathered.at[pl.ds(pl.multiple_of(source * 8, 8), 8)]
        pltpu.make_async_remote_copy(
            src_ref=summed.at[0, 0],
            dst_ref=lines,
            send_sem=out_send.at[0, 0],
            recv_sem=out_recv.at[source],
            device_id=(source, me),
            device_id_type=MESH,
        ).wait_recv()
        return carried

    lax.fori_loop(1, req_count, arrived, 0)


def spread(queries, new_keys, new_values, cached_keys, cached_values, lengths, weight):
    requests, span, q_width = queries.shape
    slots, kv_width = cached_keys.shape[1:]
    key_heads = kv_width // HEAD_SIZE
    members = q_width // kv_width
    width = weight.shape[1]
    req_count, head_count = lax.axis_size("req"), lax.axis_size("head")
    chunks = 4
    blocks = req_count // chunks
    tile = blocks * 16
    lines = blocks * 8
    loads = requests * (3 + 2 * key_heads) + 1
    anywhere = pl.BlockSpec(memory_space=pl.ANY)
    dma = pltpu.SemaphoreType.DMA
    return pl.pallas_call(
        functools.partial(spread_kernel, (req_count, head_count, requests, key_heads, members)),
        in_specs=[pl.BlockSpec(memory_space=pltpu.SMEM)] + [anywhere] * 6,
        out_specs=anywhere,
        out_shape=jax.ShapeDtypeStruct((req_count * 8, width), BF16),
        scratch_shapes=[
            pltpu.VMEM((requests, blocks, span // blocks, q_width), BF16),
            pltpu.VMEM((requests, span, kv_width), BF16),
            pltpu.VMEM((requests, slots, kv_width), BF16),
            pltpu.VMEM((requests, key_heads, slots + span, 2 * HEAD_SIZE), BF16),
            pltpu.VMEM(weight.shape, BF16),
            pltpu.VMEM((requests, tile, q_width), F32),
            pltpu.VMEM((requests * tile, q_width), BF16),
            pltpu.VMEM((chunks, head_count, lines, width), BF16),
            pltpu.VMEM((chunks, 2, lines, width // 2), BF16),
            pltpu.VMEM((chunks, 2, lines, width), BF16),
            pltpu.VMEM((chunks, blocks, 8, width), BF16),
            dma((loads,)),
            dma((chunks, 2)),
            dma((chunks, 2)),
            dma((chunks, 2)),
            dma((chunks, 2)),
            dma((chunks, blocks)),
            dma((req_count,)),
            dma,
        ],
        compiler_params=pltpu.CompilerParams(
            collective_id=0, has_side_effects=True, vmem_limit_bytes=63 << 20
        ),
    )(
        lengths,
        queries.reshape(requests, blocks, span // blocks, q_width),
        new_keys,
        new_values,
        cached_keys,
        cached_values,
        weight,
    )


def norm_kernel(rows_ref, residual_ref, gain_ref, hidden_ref, normed_ref):
    count = rows_ref.shape[0]
    positions = residual_ref.shape[0]
    lines = residual_ref.shape[1]
    target = lax.broadcasted_iota(jnp.int32, (count, count), 0)
    source = lax.broadcasted_iota(jnp.int32, (count, count), 1)
    wanted = (target & (lines - 1)) * positions + (target >> 3)
    pick = (source == wanted).astype(F32).astype(BF16)
    moved = jnp.dot(pick, rows_ref[...], preferred_element_type=F32)
    summed = residual_ref[...].astype(F32) + moved.reshape(residual_ref.shape)
    hidden_ref[...] = summed.astype(BF16)
    mean_square = jnp.mean(summed * summed, axis=-1, keepdims=True)
    scale = lax.rsqrt(mean_square + 1e-05)
    normed_ref[...] = (summed * scale * gain_ref[...].astype(F32)).astype(BF16)


def body(
    queries,
    new_keys,
    incoming_values,
    request_cached_keys,
    request_cached_values,
    cache_lengths,
    out_weight,
    residual,
    norm_gain,
):
    gathered = spread(
        queries,
        new_keys,
        incoming_values,
        request_cached_keys,
        request_cached_values,
        cache_lengths,
        out_weight,
    )
    positions, requests, width = residual.shape
    lines = 8
    block = pl.BlockSpec((positions, lines, width), lambda i: (0, i, 0))
    out = jax.ShapeDtypeStruct(residual.shape, BF16)
    hidden, normed = pl.pallas_call(
        norm_kernel,
        grid=(requests // lines,),
        in_specs=[
            pl.BlockSpec((positions * lines, width), lambda i: (i, 0)),
            block,
            pl.BlockSpec((1, 1, width), lambda i: (0, 0, 0)),
        ],
        out_specs=[block, block],
        out_shape=[out, out],
        compiler_params=pltpu.CompilerParams(vmem_limit_bytes=40 << 20),
    )(gathered, residual, norm_gain.reshape(1, 1, width))
    return hidden, normed


def solution(mesh):
    placed = (
        P("req", None, "head"),
        P("req", None, "head"),
        P("req", None, "head"),
        P("req", None, "head"),
        P("req", None, "head"),
        P("req"),
        P("head", None),
        P(("req", "head"), None, None),
        P(),
    )
    return jax.shard_map(
        body,
        mesh=mesh,
        in_specs=placed,
        out_specs=(P(("req", "head"), None, None), P(("req", "head"), None, None)),
        check_vma=False,
    )
```

time: 207 us -> 109 us (0.53)
  waiting for transfers between devices: 112 us -> 0 us
  Pallas kernels: 31.6 us -> 104 us
  local copies, waits for them, and re-layouts: 21.1 us -> 3.88 us
  matrix products: 14.2 us -> 0 us
  between operations: 14.1 us -> 0.65 us
  starting transfers between devices: 7.82 us -> 0 us
  other arithmetic: 5.81 us -> 0 us
    reduce_scatter x1 -> x0, waiting for transfers between devices: 83.9 us -> none  [body(): lax.psum_scatter(row_product(flat_rows, out_weight).astype(jnp.bfloat16),...]
    pallas_call x1 -> x2, Pallas kernels: 31.6 us -> 104 us  [the longest x1 98.9 us: spread(): pl.pallas_call(functools.partial(spread_kernel, (req_count, head_count, r...]
    all_to_all x1 -> x0, waiting for transfers between devices: 28.3 us -> none  [body(): lax.all_to_all(summed.reshape(req_count, piece_len, req_local, -1), 'req'...]
    reshape x5 -> x1, local copies, waits for them, and re-layouts: 17.2 us -> 0.71 us  [body(): norm_gain.reshape(1, 1, width)]
    dot_general x1 -> x0, matrix products: 14.2 us -> none  [row_product(): return jnp.dot(flat_rows, out_weight, preferred_element_type=jnp.float32)]
    all_to_all x1 -> x0, starting transfers between devices: 7.79 us -> none  [body(): lax.all_to_all(summed.reshape(req_count, piece_len, req_local, -1), 'req'...]
    all_to_all x1 -> x0, local copies, waits for them, and re-layouts: 3.91 us -> none  [body(): lax.all_to_all(summed.reshape(req_count, piece_len, req_local, -1), 'req'...]
    convert_element_type x2 -> x0, other arithmetic: 3.3 us -> none  [the longest x1 3.3 us: body(): (summed_rows * lax.rsqrt(mean_square + 1e-05) * norm_gain.astype(jnp.floa...]
  transfers between devices with their start and end apart: 2 -> 0, of which waited for: 2 -> 0; matrix products, arithmetic and copies ran while one was open for 0% -> 0% of each run, Pallas kernels for 0% -> 0%
where the time goes in v1:
time: 109 us; the launch traced here: 108 us
  Pallas kernels  104 us (95%)
  local copies, waits for them, and re-layouts  3.88 us (4%)
    pallas_call x1, Pallas kernels, spread(): pl.pallas_call(functools.partial(spread_kernel, (req_count, head_count, r...  98.9 us
    pallas_call x1, Pallas kernels, body(): pl.pallas_call(norm_kernel, grid=(requests // lines,), in_specs=[pl.Block...  4.79 us
    unnamed x4, local copies, waits for them, and re-layouts  3.17 us

profile of v1, /device:TPU:1, one launch (start us, length us, event | category | flops | bytes accessed | tf_op | source)
XLA Modules:
  0.0 108.3 jit_solution(5071100874427104884)
XLA Ops:
  0.6 0.7 reshape.11.gain_ref
  1.3 98.9 %shard_map.104.rows_ref = bf16[256,4096]{1,0:T(8,128)(2,1)} custom-call(s32[2]{0:T(128)} %length_ref.1, bf16[2,8,64,1024]{3,2,1,0:T(8,128)(2,1)} %bitcast.1, bf16[2,512,256]{2,1,0:T(8,128)(2,1)} %new_k_hbm.1, bf16[2,512,256]{2,1,0:T(8,128)(2,1)} %new_v_hbm.1, bf16[2,2048,256]{2,1,0:T(8,128)(2,1)} %key_hbm.1, bf16[2,2048,256]{2,1,0:T(8,128)(2,1)} %value_hbm.1, ...), custom_call_target="tpu_custom_call" | custom-call | tf_op jit(solution)/shard_map/pallas_call | solution.py:286
  100.3 0.0 copy-start
  100.3 1.6 %copy-done = bf16[256,4096]{1,0:T(8,128)(2,1)S(1)} copy-done((bf16[256,4096]{1,0:T(8,128)(2,1)S(1)}, bf16[256,4096]{1,0:T(8,128)(2,1)}, u32[]{:S(2)}) %copy-start) | copy-done | bytes 2097176
  101.9 0.0 copy-start.1
  101.9 1.6 %copy-done.1 = bf16[4,64,4096]{2,1,0:T(8,128)(2,1)S(1)} copy-done((bf16[4,64,4096]{2,1,0:T(8,128)(2,1)S(1)}, bf16[4,64,4096]{2,1,0:T(8,128)(2,1)}, u32[]{:S(2)}) %copy-start.1) | copy-done | bytes 2097176
  103.5 4.8 %shard_map.105 = (bf16[4,64,4096]{2,1,0:T(8,128)(2,1)}, bf16[4,64,4096]{2,1,0:T(8,128)(2,1)}) custom-call(bf16[256,4096]{1,0:T(8,128)(2,1)S(1)} %copy-done, bf16[4,64,4096]{2,1,0:T(8,128)(2,1)S(1)} %copy-done.1, bf16[1,1,4096]{2,1,0:T(2,128)(2,1)S(1)} %reshape.11.gain_ref), custom_call_target="tpu_custom_call" | custom-call | tf_op jit(solution)/shard_map/pallas_call | solution.py:366
Async XLA Ops:
  100.3 1.6 %copy-start = (bf16[256,4096]{1,0:T(8,128)(2,1)S(1)}, bf16[256,4096]{1,0:T(8,128)(2,1)}, u32[]{:S(2)}) copy-start(bf16[256,4096]{1,0:T(8,128)(2,1)} %shard_map.104.rows_ref) | copy-start | bytes 6291460
  101.9 1.6 %copy-start.1 = (bf16[4,64,4096]{2,1,0:T(8,128)(2,1)S(1)}, bf16[4,64,4096]{2,1,0:T(8,128)(2,1)}, u32[]{:S(2)}) copy-start(bf16[4,64,4096]{2,1,0:T(8,128)(2,1)} %residual_ref.1) | copy-start | bytes 6291460

commit v2 on v1

--- a/solution.py
+++ b/solution.py
@@ -39,6 +39,7 @@
     near_in,
     summed,
     load_sem,
+    weight_sem,
     far_send,
     far_recv,
     near_send,
@@ -74,22 +75,26 @@
         for g in range(key_heads):
             values[r, g, :, HEAD_SIZE:] = jnp.ones((slots + span, HEAD_SIZE), BF16)
 
-    loads = []
-
-    def load(source, target):
-        copy = pltpu.make_async_copy(source, target, load_sem.at[len(loads)])
-        copy.start()
-        loads.append(copy)
+    def loads(r):
+        pairs = [
+            (q_hbm.at[r], query.at[r]),
+            (key_hbm.at[r], keys.at[r]),
+            (new_k_hbm.at[r], new_keys.at[r]),
+        ]
+        for g, lanes in enumerate(lane_groups):
+            old = values.at[r, g, pl.ds(0, slots), pl.ds(0, HEAD_SIZE)]
+            new = values.at[r, g, pl.ds(slots, span), pl.ds(0, HEAD_SIZE)]
+            pairs += [(value_hbm.at[r, :, lanes], old), (new_v_hbm.at[r, :, lanes], new)]
+        return [
+            pltpu.make_async_copy(source, target, load_sem.at[r, i])
+            for i, (source, target) in enumerate(pairs)
+        ]
 
     for r in range(requests):
-        load(q_hbm.at[r], query.at[r])
-        load(key_hbm.at[r], keys.at[r])
-        load(new_k_hbm.at[r], new_keys.at[r])
-        for g, lanes in enumerate(lane_groups):
-            load(value_hbm.at[r, :, lanes], values.at[r, g, pl.ds(0, slots), pl.ds(0, HEAD_SIZE)])
-            load(new_v_hbm.at[r, :, lanes], values.at[r, g, pl.ds(slots, span), pl.ds(0, HEAD_SIZE)])
-    load(weight_hbm, weight)
-    per_request = (len(loads) - 1) // requests
+        for copy in loads(r):
+            copy.start()
+    weight_load = pltpu.make_async_copy(weight_hbm, weight, weight_sem)
+    weight_load.start()
 
     contract_last = (((1,), (1,)), ((), ()))
 
@@ -98,10 +103,11 @@
         tile = query.shape[1] * 16
         stacked = members * tile
         for g in range(key_heads):
-            block = query[r, :, pl.ds(pl.multiple_of(turn * 16, 16), 16), pl.ds(g * members * HEAD_SIZE, members * HEAD_SIZE)]
-            block = block.reshape(tile, members * HEAD_SIZE)
+            lanes = pl.ds(g * members * HEAD_SIZE, members * HEAD_SIZE)
+            rows = query[r, :, pl.ds(pl.multiple_of(turn * 16, 16), 16), lanes]
+            rows = rows.reshape(tile, members * HEAD_SIZE)
             q = jnp.concatenate(
-                [block[:, j * HEAD_SIZE : (j + 1) * HEAD_SIZE] for j in range(members)], axis=0
+                [rows[:, j * HEAD_SIZE : (j + 1) * HEAD_SIZE] for j in range(members)], axis=0
             )
             running_max = total = None
             for at in range(0, slots + span, K_BLOCK):
@@ -116,7 +122,8 @@
                     scores = scores + jnp.where(slot < length, 0.0, NEGATIVE_FILLER)
                 else:
                     line = lax.broadcasted_iota(jnp.int32, (stacked, K_BLOCK), 0)
-                    position = ((line >> 4) & 7) * 64 + (line & 15) + turn * 16
+                    block = (line >> 4) & (query.shape[1] - 1)
+                    position = block * query.shape[2] + (line & 15) + turn * 16
                     column = lax.broadcasted_iota(jnp.int32, (stacked, K_BLOCK), 1) + (at - slots)
                     scores = jnp.where(column <= position, scores, NEGATIVE_FILLER)
                 block_max = jnp.max(scores, axis=1, keepdims=True)
@@ -167,13 +174,14 @@
             device_id_type=MESH,
         )
 
-    def near(c, side):
+    def near(c, side, summed_half):
         target = (right, left)[side]
+        columns = pl.ds((side if summed_half else 1 - side) * half, half)
         return pltpu.make_async_remote_copy(
-            src_ref=part.at[c, target],
-            dst_ref=near_in.at[c, side],
-            send_sem=near_send.at[c, side],
-            recv_sem=near_recv.at[c, side],
+            src_ref=part.at[c, target, :, columns],
+            dst_ref=near_in.at[c, side, :, columns],
+            send_sem=near_send.at[c, side, int(summed_half)],
+            recv_sem=near_recv.at[c, side, int(summed_half)],
             device_id=(row, target),
             device_id_type=MESH,
         )
@@ -184,14 +192,15 @@
             columns = pl.ds(side * half, half)
             own = part[c, target, :, columns].astype(F32)
             part[c, target, :, columns] = (own + far_in[c, side].astype(F32)).astype(BF16)
-            near(c, side).start()
+            near(c, side, True).start()
 
     group, place = row // chunks, lax.rem(row, chunks)
     groups = req_count // chunks
 
-    def finish(c):
+    def finish(c, kept=False):
         for side in range(2):
-            near(c, side).wait_recv()
+            near(c, side, False).wait_recv()
+            near(c, side, True).wait_recv()
         total = part[c, me].astype(F32) + near_in[c, 0].astype(F32) + near_in[c, 1].astype(F32)
         summed[c] = total.reshape(summed.shape[1:]).astype(BF16)
 
@@ -199,9 +208,9 @@
             outgoing(c, step).start()
             return carried
 
-        if c == 0:
+        if kept:
             keep().start()
-        lax.fori_loop(1 if c == 0 else 0, groups, send, 0)
+        lax.fori_loop(1 if kept else 0, groups, send, 0)
 
     def outgoing(c, step):
         block = lax.rem(group + step, groups)
@@ -219,33 +228,50 @@
         lines = gathered.at[pl.ds(pl.multiple_of(row * 8, 8), 8)]
         return pltpu.make_async_copy(summed.at[0, group], lines, self_sem)
 
-    for c in range(chunks):
-        turn = lax.rem(place + c, chunks)
-        for r in range(requests):
-            if c == 0:
-                for copy in loads[r * per_request : (r + 1) * per_request]:
-                    copy.wait()
-            attend(turn, r)
-            if c > 0 and r == 0:
-                pass_on(c - 1)
-        if c > 1:
-            finish(c - 2)
-        order_rows()
-        if c == 0:
-            loads[-1].wait()
+    def half_chunk(step, carried):
+        c, r = lax.div(step, requests), lax.rem(step, requests)
+
+        @pl.when(c == 0)
+        def _():
+            for copy in loads(r):
+                copy.wait()
+
+        @pl.when(step == 1)
+        def _():
             pl.semaphore_wait(barrier, 2 + req_count - 1)
-        for side in range(2):
-            project(c, side)
-            far(c, side).start()
+
+        attend(lax.rem(place + c, chunks), r)
+
+        @pl.when(r == requests - 1)
+        def _():
+            pl.when(c > 0)(lambda: pass_on(c - 1))
+            order_rows()
+
+            @pl.when(c == 0)
+            def _():
+                weight_load.wait()
+
+            for side in range(2):
+                project(c, side)
+                far(c, side).start()
+            for side in range(2):
+                near(c, side, False).start()
+            pl.when(c == 2)(lambda: finish(0, True))
+            pl.when(c > 2)(lambda: finish(c - 2))
+
+        return carried
+
+    lax.fori_loop(0, chunks * requests, half_chunk, 0)
+    finish(chunks - 2)
     pass_on(chunks - 1)
-    for c in range(max(0, chunks - 2), chunks):
-        finish(c)
+    finish(chunks - 1)
 
     keep().wait()
     for c in range(chunks):
         for side in range(2):
             far(c, side).wait_send()
-            near(c, side).wait_send()
+            near(c, side, False).wait_send()
+            near(c, side, True).wait_send()
 
         def sent(step, carried, c=c):
             outgoing(c, step).wait_send()
@@ -276,11 +302,10 @@
     members = q_width // kv_width
     width = weight.shape[1]
     req_count, head_count = lax.axis_size("req"), lax.axis_size("head")
-    chunks = 4
+    chunks = 8
     blocks = req_count // chunks
     tile = blocks * 16
     lines = blocks * 8
-    loads = requests * (3 + 2 * key_heads) + 1
     anywhere = pl.BlockSpec(memory_space=pl.ANY)
     dma = pltpu.SemaphoreType.DMA
     return pl.pallas_call(
@@ -300,11 +325,12 @@
             pltpu.VMEM((chunks, 2, lines, width // 2), BF16),
             pltpu.VMEM((chunks, 2, lines, width), BF16),
             pltpu.VMEM((chunks, blocks, 8, width), BF16),
-            dma((loads,)),
+            dma((requests, 3 + 2 * key_heads)),
+            dma,
             dma((chunks, 2)),
             dma((chunks, 2)),
-            dma((chunks, 2)),
-            dma((chunks, 2)),
+            dma((chunks, 2, 2)),
+            dma((chunks, 2, 2)),
             dma((chunks, blocks)),
             dma((req_count,)),
             dma,
@@ -329,14 +355,14 @@
     lines = residual_ref.shape[1]
     target = lax.broadcasted_iota(jnp.int32, (count, count), 0)
     source = lax.broadcasted_iota(jnp.int32, (count, count), 1)
-    wanted = (target & (lines - 1)) * positions + (target >> 3)
+    wanted = (target & (lines - 1)) * positions + (target >> (lines.bit_length() - 1))
     pick = (source == wanted).astype(F32).astype(BF16)
     moved = jnp.dot(pick, rows_ref[...], preferred_element_type=F32)
     summed = residual_ref[...].astype(F32) + moved.reshape(residual_ref.shape)
     hidden_ref[...] = summed.astype(BF16)
     mean_square = jnp.mean(summed * summed, axis=-1, keepdims=True)
     scale = lax.rsqrt(mean_square + 1e-05)
-    normed_ref[...] = (summed * scale * gain_ref[...].astype(F32)).astype(BF16)
+    normed_ref[...] = (summed * scale * gain_ref[...].astype(F32)[None, None]).astype(BF16)
 
 
 def body(
@@ -360,7 +386,7 @@
         out_weight,
     )
     positions, requests, width = residual.shape
-    lines = 8
+    lines = 32
     block = pl.BlockSpec((positions, lines, width), lambda i: (0, i, 0))
     out = jax.ShapeDtypeStruct(residual.shape, BF16)
     hidden, normed = pl.pallas_call(
@@ -369,12 +395,12 @@
         in_specs=[
             pl.BlockSpec((positions * lines, width), lambda i: (i, 0)),
             block,
-            pl.BlockSpec((1, 1, width), lambda i: (0, 0, 0)),
+            pl.BlockSpec((width,), lambda i: (0,)),
         ],
         out_specs=[block, block],
         out_shape=[out, out],
-        compiler_params=pltpu.CompilerParams(vmem_limit_bytes=40 << 20),
-    )(gathered, residual, norm_gain.reshape(1, 1, width))
+        compiler_params=pltpu.CompilerParams(vmem_limit_bytes=63 << 20),
+    )(gathered, residual, norm_gain)
     return hidden, normed
 
 

time: 109 us -> 95.7 us (0.88)
  Pallas kernels: 104 us -> 94.9 us
  local copies, waits for them, and re-layouts: 3.88 us -> 0 us
    pallas_call x1, Pallas kernels: 98.9 us -> 90.5 us  [spread(): pl.pallas_call(functools.partial(spread_kernel, (req_count, head_count, r...]
    unnamed x4 -> x0, local copies, waits for them, and re-layouts: 3.17 us -> none
where the time goes in v2:
time: 95.7 us; the launch traced here: 95.6 us
  Pallas kernels  94.9 us (99%)
    pallas_call x1, Pallas kernels, spread(): pl.pallas_call(functools.partial(spread_kernel, (req_count, head_count, r...  90.5 us
    pallas_call x1, Pallas kernels, body(): pl.pallas_call(norm_kernel, grid=(requests // lines,), in_specs=[pl.Block...  4.42 us

profile of v2, /device:TPU:1, one launch (start us, length us, event | category | flops | bytes accessed | tf_op | source)
XLA Modules:
  0.0 95.6 jit_solution(17950537948221629571)
XLA Ops:
  0.6 90.5 %shard_map.104.rows_ref = bf16[256,4096]{1,0:T(8,128)(2,1)} custom-call(s32[2]{0:T(128)} %length_ref.1, bf16[2,4,128,1024]{3,2,1,0:T(8,128)(2,1)} %bitcast.1, bf16[2,512,256]{2,1,0:T(8,128)(2,1)} %new_k_hbm.1, bf16[2,512,256]{2,1,0:T(8,128)(2,1)} %new_v_hbm.1, bf16[2,2048,256]{2,1,0:T(8,128)(2,1)} %key_hbm.1, bf16[2,2048,256]{2,1,0:T(8,128)(2,1)} %value_hbm.1, ...), custom_call_target="tpu_custom_call" | custom-call | tf_op jit(solution)/shard_map/pallas_call | solution.py:311
  91.2 4.4 %shard_map.105 = (bf16[4,64,4096]{2,1,0:T(8,128)(2,1)}, bf16[4,64,4096]{2,1,0:T(8,128)(2,1)}) custom-call(bf16[256,4096]{1,0:T(8,128)(2,1)} %shard_map.104.rows_ref, bf16[4,64,4096]{2,1,0:T(8,128)(2,1)} %residual_ref.1, bf16[4096]{0:T(1024)(128)(2,1)} %gain_ref.1), custom_call_target="tpu_custom_call" | custom-call | tf_op jit(solution)/shard_map/pallas_call | solution.py:392

commit v3 on v2

--- a/solution.py
+++ b/solution.py
@@ -32,14 +32,25 @@
     keys,
     values,
     weight,
+    pair_weight,
     attended,
     rows_of_owner,
     part,
     far_in,
     near_in,
+    pair_rows,
+    mixed,
+    wide_part,
+    wide_in,
     summed,
     load_sem,
     weight_sem,
+    piece_send,
+    piece_recv,
+    rows_send,
+    rows_recv,
+    wide_send,
+    wide_recv,
     far_send,
     far_recv,
     near_send,
@@ -51,17 +62,18 @@
     req_count, head_count, requests, key_heads, members = sizes
     row = lax.axis_index("req")
     me = lax.axis_index("head")
-    right = lax.rem(me + 1, head_count)
-    left = lax.rem(me + head_count - 1, head_count)
-    opposite = lax.rem(me + 2, head_count)
+    pair = me + 1 - 2 * lax.rem(me, 2)
+    across = head_count - 1 - me
+    opposite = head_count - 1 - pair
+    sides = (pair, across)
     chunks = part.shape[0]
     slots, span = key_hbm.shape[1], new_k_hbm.shape[1]
-    width = weight.shape[1]
-    half = width // 2
+    narrow = part.shape[3]
+    half = narrow // 2
     lane_groups = [pl.ds(g * HEAD_SIZE, HEAD_SIZE) for g in range(key_heads)]
 
     barrier = pltpu.get_barrier_semaphore()
-    for neighbour in (left, right):
+    for neighbour in sides:
         pl.semaphore_signal(barrier, inc=1, device_id=(row, neighbour), device_id_type=MESH)
 
     def greet(step, carried):
@@ -95,6 +107,82 @@
             copy.start()
     weight_load = pltpu.make_async_copy(weight_hbm, weight, weight_sem)
     weight_load.start()
+
+    depth = weight.shape[0] // 2
+    share = depth // req_count
+    core = lax.rem(row, 2)
+    sibling = row + 1 - 2 * core
+
+    def place_of(along_y, along_z):
+        y = lax.rem(row // 8 + along_y, 4)
+        z = lax.rem(lax.rem(row // 2, 4) + along_z, 4)
+        return y * 8 + z * 2 + core
+
+    def along(order, first, second):
+        return place_of(first, second) if order == 0 else place_of(second, first)
+
+    def give(order, piece, slot, device, source=None):
+        lines = pl.ds(pl.multiple_of(order * depth + piece * share, share), share)
+        return pltpu.make_async_remote_copy(
+            src_ref=pair_weight.at[lines] if source is None else weight_hbm.at[lines, pl.ds(narrow, narrow)],
+            dst_ref=pair_weight.at[lines],
+            send_sem=piece_send.at[order, slot],
+            recv_sem=piece_recv.at[order, piece],
+            device_id=device,
+            device_id_type=MESH,
+        )
+
+    def take(order, piece):
+        give(order, piece, 0, (sibling, me)).wait_recv()
+
+    def fetch_pieces():
+        for order in range(2):
+            give(order, row, 0, (row, pair), weight_hbm).start()
+
+    def first_line():
+        for order in range(2):
+            take(order, row)
+            for k in range(1, 4):
+                give(order, row, k, (along(order, k, 0), me)).start()
+
+    def second_line():
+        for order in range(2):
+            for j in range(4):
+                piece = along(order, j, 0)
+                if j:
+                    take(order, piece)
+                for k in range(1, 4):
+                    give(order, piece, 3 + j * 3 + k, (along(order, 0, k), me)).start()
+
+    def to_sibling():
+        for order in range(2):
+
+            def one(n, carried, order=order):
+                piece = along(order, lax.rem(n, 4), n // 4)
+                pl.when(n >= 4)(lambda: take(order, piece))
+                give(order, piece, 16 + n, (sibling, me)).start()
+                return carried
+
+            lax.fori_loop(0, 16, one, 0)
+
+    def from_sibling():
+        for order in range(2):
+
+            def one(n, carried, order=order):
+                take(order, along(order, lax.rem(n, 4), n // 4) + 1 - 2 * core)
+                return carried
+
+            lax.fori_loop(0, 16, one, 0)
+
+    def pieces_sent():
+        for order in range(2):
+            give(order, row, 0, (row, pair), weight_hbm).wait_send()
+
+            def one(n, carried, order=order):
+                give(order, row, n, (sibling, me)).wait_send()
+                return carried
+
+            lax.fori_loop(1, 32, one, 0)
 
     contract_last = (((1,), (1,)), ((), ()))
 
@@ -140,7 +228,7 @@
                 at = (g * members + j) * HEAD_SIZE
                 attended[r, :, at : at + HEAD_SIZE] = out[j * tile : (j + 1) * tile]
 
-    def order_rows():
+    def order_rows(c):
         count = attended.shape[1] // 8
         shape = (count, 8, attended.shape[2])
         first, second = attended[0].reshape(shape), attended[1].reshape(shape)
@@ -152,17 +240,63 @@
             for high in range(2):
                 owner = 2 * high + low
                 lines = split[:, high].reshape(count * 4, shape[2]).astype(BF16)
-                rows_of_owner[owner * count * 4 : (owner + 1) * count * 4] = lines
+                rows_of_owner[c, owner] = lines
 
     def project(c, first):
         def tile(n, carried):
             columns = pl.ds(pl.multiple_of(n * N_TILE, N_TILE), N_TILE)
-            product = jnp.dot(rows_of_owner[...], weight[:, columns], preferred_element_type=F32)
+            rows = rows_of_owner[c].reshape(-1, weight.shape[0])
+            product = jnp.dot(rows, weight[:, columns], preferred_element_type=F32)
             part[c, :, :, columns] = product.astype(BF16).reshape(head_count, -1, N_TILE)
             return carried
 
         tiles = half // N_TILE
         lax.fori_loop(first * tiles, (first + 1) * tiles, tile, 0)
+
+    def lend(c, which):
+        return pltpu.make_async_remote_copy(
+            src_ref=rows_of_owner.at[c, (pair, opposite)[which]],
+            dst_ref=pair_rows.at[c, which],
+            send_sem=rows_send.at[c, which],
+            recv_sem=rows_recv.at[c, which],
+            device_id=(row, pair),
+            device_id_type=MESH,
+        )
+
+    def hand_across(c):
+        return pltpu.make_async_remote_copy(
+            src_ref=wide_part.at[c, 1],
+            dst_ref=wide_in.at[c],
+            send_sem=wide_send.at[c],
+            recv_sem=wide_recv.at[c],
+            device_id=(row, across),
+            device_id_type=MESH,
+        )
+
+    def project_both(pairing, carried):
+        inner = weight.shape[0]
+        lines = rows_of_owner.shape[2]
+        for i in range(2):
+            c = 2 * pairing + i
+            for which, owner in enumerate((me, across)):
+                lend(c, which).wait_recv()
+                at = (2 * i + which) * lines
+                mixed[at : at + lines, :inner] = rows_of_owner[c, owner]
+                mixed[at : at + lines, inner:] = pair_rows[c, which]
+
+        def tile(n, inner_carried):
+            columns = pl.ds(pl.multiple_of(n * N_TILE, N_TILE), N_TILE)
+            own_columns = pl.ds(pl.multiple_of(narrow + n * N_TILE, N_TILE), N_TILE)
+            product = jnp.dot(mixed[:, :inner], weight[:, own_columns], preferred_element_type=F32)
+            product += jnp.dot(mixed[:, inner:], pair_weight[:, columns], preferred_element_type=F32)
+            block = product.astype(BF16).reshape(2, 2, lines, N_TILE)
+            wide_part[pl.ds(2 * pairing, 2), :, :, columns] = block
+            return inner_carried
+
+        lax.fori_loop(0, narrow // N_TILE, tile, 0)
+        for i in range(2):
+            hand_across(2 * pairing + i).start()
+        return carried
 
     def far(c, side):
         return pltpu.make_async_remote_copy(
@@ -170,29 +304,34 @@
             dst_ref=far_in.at[c, side],
             send_sem=far_send.at[c, side],
             recv_sem=far_recv.at[c, side],
-            device_id=(row, (right, left)[side]),
+            device_id=(row, sides[side]),
             device_id_type=MESH,
         )
 
     def near(c, side, summed_half):
-        target = (right, left)[side]
-        columns = pl.ds((side if summed_half else 1 - side) * half, half)
+        columns = pl.ds((1 - side if summed_half else side) * half, half)
         return pltpu.make_async_remote_copy(
-            src_ref=part.at[c, target, :, columns],
+            src_ref=part.at[c, sides[side], :, columns],
             dst_ref=near_in.at[c, side, :, columns],
             send_sem=near_send.at[c, side, int(summed_half)],
             recv_sem=near_recv.at[c, side, int(summed_half)],
-            device_id=(row, target),
+            device_id=(row, sides[side]),
             device_id_type=MESH,
         )
 
     def pass_on(c):
-        for side, target in enumerate((right, left)):
+        for side in range(2):
             far(c, side).wait_recv()
+            target = sides[1 - side]
             columns = pl.ds(side * half, half)
             own = part[c, target, :, columns].astype(F32)
             part[c, target, :, columns] = (own + far_in[c, side].astype(F32)).astype(BF16)
-            near(c, side, True).start()
+            if side == 0:
+                near(c, 1, True).start()
+
+    def to_pair(c):
+        near(c, 0, False).start()
+        near(c, 0, True).start()
 
     group, place = row // chunks, lax.rem(row, chunks)
     groups = req_count // chunks
@@ -202,7 +341,11 @@
             near(c, side, False).wait_recv()
             near(c, side, True).wait_recv()
         total = part[c, me].astype(F32) + near_in[c, 0].astype(F32) + near_in[c, 1].astype(F32)
-        summed[c] = total.reshape(summed.shape[1:]).astype(BF16)
+        shape = summed.shape[1:3] + (narrow,)
+        summed[c, :, :, :narrow] = total.reshape(shape).astype(BF16)
+        hand_across(c).wait_recv()
+        total = wide_part[c, 0].astype(F32) + wide_in[c].astype(F32)
+        summed[c, :, :, narrow:] = total.reshape(shape).astype(BF16)
 
         def send(step, carried):
             outgoing(c, step).start()
@@ -231,21 +374,28 @@
     def half_chunk(step, carried):
         c, r = lax.div(step, requests), lax.rem(step, requests)
 
+        @pl.when(step == 0)
+        def _():
+            pl.semaphore_wait(barrier, 2 + req_count - 1)
+            fetch_pieces()
+
+        pl.when(step == 2)(first_line)
+        pl.when(step == 5)(second_line)
+        pl.when(step == 12)(to_sibling)
+
         @pl.when(c == 0)
         def _():
             for copy in loads(r):
                 copy.wait()
 
-        @pl.when(step == 1)
-        def _():
-            pl.semaphore_wait(barrier, 2 + req_count - 1)
-
         attend(lax.rem(place + c, chunks), r)
 
         @pl.when(r == requests - 1)
         def _():
             pl.when(c > 0)(lambda: pass_on(c - 1))
-            order_rows()
+            order_rows(c)
+            for which in range(2):
+                lend(c, which).start()
 
             @pl.when(c == 0)
             def _():
@@ -254,24 +404,39 @@
             for side in range(2):
                 project(c, side)
                 far(c, side).start()
-            for side in range(2):
-                near(c, side, False).start()
-            pl.when(c == 2)(lambda: finish(0, True))
-            pl.when(c > 2)(lambda: finish(c - 2))
+            near(c, 1, False).start()
 
         return carried
 
     lax.fori_loop(0, chunks * requests, half_chunk, 0)
-    finish(chunks - 2)
+
+    def early(c, carried):
+        to_pair(c)
+        return carried
+
+    lax.fori_loop(0, chunks - 1, early, 0)
+    from_sibling()
+    lax.fori_loop(0, chunks // 4, project_both, 0)
     pass_on(chunks - 1)
-    finish(chunks - 1)
+    to_pair(chunks - 1)
+    lax.fori_loop(chunks // 4, chunks // 2, project_both, 0)
+    finish(0, True)
+
+    def rest(c, carried):
+        finish(c)
+        return carried
+
+    lax.fori_loop(1, chunks, rest, 0)
 
     keep().wait()
+    pieces_sent()
     for c in range(chunks):
         for side in range(2):
+            lend(c, side).wait_send()
             far(c, side).wait_send()
             near(c, side, False).wait_send()
             near(c, side, True).wait_send()
+        hand_across(c).wait_send()
 
         def sent(step, carried, c=c):
             outgoing(c, step).wait_send()
@@ -306,6 +471,7 @@
     blocks = req_count // chunks
     tile = blocks * 16
     lines = blocks * 8
+    narrow = width // 2
     anywhere = pl.BlockSpec(memory_space=pl.ANY)
     dma = pltpu.SemaphoreType.DMA
     return pl.pallas_call(
@@ -319,14 +485,25 @@
             pltpu.VMEM((requests, slots, kv_width), BF16),
             pltpu.VMEM((requests, key_heads, slots + span, 2 * HEAD_SIZE), BF16),
             pltpu.VMEM(weight.shape, BF16),
+            pltpu.VMEM((q_width, narrow), BF16),
             pltpu.VMEM((requests, tile, q_width), F32),
-            pltpu.VMEM((requests * tile, q_width), BF16),
-            pltpu.VMEM((chunks, head_count, lines, width), BF16),
-            pltpu.VMEM((chunks, 2, lines, width // 2), BF16),
-            pltpu.VMEM((chunks, 2, lines, width), BF16),
+            pltpu.VMEM((chunks, head_count, lines, q_width), BF16),
+            pltpu.VMEM((chunks, head_count, lines, narrow), BF16),
+            pltpu.VMEM((chunks, 2, lines, narrow // 2), BF16),
+            pltpu.VMEM((chunks, 2, lines, narrow), BF16),
+            pltpu.VMEM((chunks, 2, lines, q_width), BF16),
+            pltpu.VMEM((4 * lines, 2 * q_width), BF16),
+            pltpu.VMEM((chunks, 2, lines, narrow), BF16),
+            pltpu.VMEM((chunks, lines, narrow), BF16),
             pltpu.VMEM((chunks, blocks, 8, width), BF16),
             dma((requests, 3 + 2 * key_heads)),
             dma,
+            dma((2, 32)),
+            dma((2, req_count)),
+            dma((chunks, 2)),
+            dma((chunks, 2)),
+            dma((chunks,)),
+            dma((chunks,)),
             dma((chunks, 2)),
             dma((chunks, 2)),
             dma((chunks, 2, 2)),

time: 95.7 us -> 105 us (1.097)
  Pallas kernels: 94.9 us -> 104 us
    pallas_call x1, Pallas kernels: 90.5 us -> 99.8 us  [spread(): pl.pallas_call(functools.partial(spread_kernel, (req_count, head_count, r...]
where the time goes in v3:
time: 105 us
  Pallas kernels  104 us (99%)
    pallas_call x1, Pallas kernels, spread(): pl.pallas_call(functools.partial(spread_kernel, (req_count, head_count, r...  99.8 us
    pallas_call x1, Pallas kernels, body(): pl.pallas_call(norm_kernel, grid=(requests // lines,), in_specs=[pl.Block...  4.43 us

profile of v3, /device:TPU:1, one launch (start us, length us, event | category | flops | bytes accessed | tf_op | source)
XLA Modules:
  0.0 104.9 jit_solution(9461332183528773975)
XLA Ops:
  0.6 99.8 %shard_map.104.rows_ref = bf16[256,4096]{1,0:T(8,128)(2,1)} custom-call(s32[2]{0:T(128)} %length_ref.1, bf16[2,4,128,1024]{3,2,1,0:T(8,128)(2,1)} %bitcast.1, bf16[2,512,256]{2,1,0:T(8,128)(2,1)} %new_k_hbm.1, bf16[2,512,256]{2,1,0:T(8,128)(2,1)} %new_v_hbm.1, bf16[2,2048,256]{2,1,0:T(8,128)(2,1)} %key_hbm.1, bf16[2,2048,256]{2,1,0:T(8,128)(2,1)} %value_hbm.1, ...), custom_call_target="tpu_custom_call" | custom-call | tf_op jit(solution)/shard_map/pallas_call | solution.py:477
  100.5 4.4 %shard_map.105 = (bf16[4,64,4096]{2,1,0:T(8,128)(2,1)}, bf16[4,64,4096]{2,1,0:T(8,128)(2,1)}) custom-call(bf16[256,4096]{1,0:T(8,128)(2,1)} %shard_map.104.rows_ref, bf16[4,64,4096]{2,1,0:T(8,128)(2,1)} %residual_ref.1, bf16[4096]{0:T(1024)(128)(2,1)} %gain_ref.1), custom_call_target="tpu_custom_call" | custom-call | tf_op jit(solution)/shard_map/pallas_call | solution.py:569

commit v4 on v3

--- a/solution.py
+++ b/solution.py
@@ -416,17 +416,22 @@
 
     lax.fori_loop(0, chunks - 1, early, 0)
     from_sibling()
-    lax.fori_loop(0, chunks // 4, project_both, 0)
+    project_both(0, 0)
     pass_on(chunks - 1)
     to_pair(chunks - 1)
-    lax.fori_loop(chunks // 4, chunks // 2, project_both, 0)
+    project_both(1, 0)
     finish(0, True)
-
-    def rest(c, carried):
-        finish(c)
+    finish(1)
+
+    def both_and_finish(pairing, carried):
+        project_both(pairing, carried)
+        finish(2 * pairing - 2)
+        finish(2 * pairing - 1)
         return carried
 
-    lax.fori_loop(1, chunks, rest, 0)
+    lax.fori_loop(2, chunks // 2, both_and_finish, 0)
+    finish(chunks - 2)
+    finish(chunks - 1)
 
     keep().wait()
     pieces_sent()

time: 105 us -> 105 us (level)
  no operation moved by 1% of the time
where the time goes in v4:
time: 105 us
  Pallas kernels  105 us (100%)
    pallas_call x1, Pallas kernels, spread(): pl.pallas_call(functools.partial(spread_kernel, (req_count, head_count, r...  100 us
    pallas_call x1, Pallas kernels, body(): pl.pallas_call(norm_kernel, grid=(requests // lines,), in_specs=[pl.Block...  4.43 us

profile of v4, /device:TPU:1, one launch (start us, length us, event | category | flops | bytes accessed | tf_op | source)
XLA Modules:
  0.0 105.3 jit_solution(10484123297277803665)
XLA Ops:
  0.6 100.2 %shard_map.104.rows_ref = bf16[256,4096]{1,0:T(8,128)(2,1)} custom-call(s32[2]{0:T(128)} %length_ref.1, bf16[2,4,128,1024]{3,2,1,0:T(8,128)(2,1)} %bitcast.1, bf16[2,512,256]{2,1,0:T(8,128)(2,1)} %new_k_hbm.1, bf16[2,512,256]{2,1,0:T(8,128)(2,1)} %new_v_hbm.1, bf16[2,2048,256]{2,1,0:T(8,128)(2,1)} %key_hbm.1, bf16[2,2048,256]{2,1,0:T(8,128)(2,1)} %value_hbm.1, ...), custom_call_target="tpu_custom_call" | custom-call | tf_op jit(solution)/shard_map/pallas_call | solution.py:482
  100.9 4.4 %shard_map.105 = (bf16[4,64,4096]{2,1,0:T(8,128)(2,1)}, bf16[4,64,4096]{2,1,0:T(8,128)(2,1)}) custom-call(bf16[256,4096]{1,0:T(8,128)(2,1)} %shard_map.104.rows_ref, bf16[4,64,4096]{2,1,0:T(8,128)(2,1)} %residual_ref.1, bf16[4096]{0:T(1024)(128)(2,1)} %gain_ref.1), custom_call_target="tpu_custom_call" | custom-call | tf_op jit(solution)/shard_map/pallas_call | solution.py:574
